TPU v7x, 32 devices: a whole 2x2x4 slice. The times are simulated.
32 devices in a mesh: space: 4 (over x, core), tile: 8 (over z, y).
Axes of the slice: x: 2, y: 2, z: 4, core: 2. Of those that a mesh axis runs over, the one named last changes fastest.
Arguments:
- atom_feat: bfloat16 [512, 128, 128], P(('space', 'tile')), may hold values from -6 to 6
- atom_pos: bfloat16 [512, 3, 128], P(('space', 'tile')), may hold values from 0 to 4
- atom_counts: int32 [512], P(('space', 'tile')), may hold values from 32 to 128
- atom_nbrs: int32 [512, 4], P(('space', 'tile')), may hold values from 0 to 511, as said below
- probe_pos: float32 [64, 3, 512], P(('space', 'tile')), may hold values from 0 to 4
- probe_target: float32 [64, 512], P(('space', 'tile')), may hold values from -6 to 6
- tile_blocks: int32 [64, 8], P(('space', 'tile')), may hold values from 0 to 511, as said below
- atom_filter: bfloat16 [128, 1024], replicated, may hold values from -0.5 to 0.5
- probe_filter: bfloat16 [128, 1024], replicated, may hold values from -0.5 to 0.5
- mix_weight: bfloat16 [128, 128], replicated, may hold values from -0.5 to 0.5
- readout: float32 [128], replicated, may hold values from -0.5 to 0.5
Outputs:
- density: float32 [64, 512], P(('space', 'tile'))
- atom_filter_grad: float32 [128, 1024], replicated
- probe_filter_grad: float32 [128, 1024], replicated
- mix_grad: float32 [128, 128], replicated
- readout_grad: float32 [128], replicated
Inputs may be any that keep to these rules, and one draw needn't show every extreme that they name: `atom_nbrs`: block g lies on device g // 16 in the order space then tile. The 4 neighbours of a block lie on devices of the same tile index whose space index differs by at most one, cyclically: the first one lower, the second one higher, the third the same; they need not be distinct. `tile_blocks`: the 8 blocks of a tile are distinct and lie on devices of the tile's own space index. The tiles of one device read at most 4 distinct blocks from any one device, and exactly 4 from some device.
All inputs are finite; a program needn't handle non-finite values.
Results may differ from a plain program's by a relative error of at most 0.0061.
Values may be sent and summed in bfloat16 or wider, within the bound.
A program may use at most 64 MiB of HBM per device.

v0:
```python
import jax
import jax.numpy as jnp
from jax import lax
from jax.sharding import PartitionSpec as P

CUTOFF = 6.0
SPACING = 0.75
SPREAD = 0.75


def with_halo(block, sides, width):
    for axis, dim in sides:
        count = lax.axis_size(axis)
        forward = [(i, i + 1) for i in range(count - 1)]
        forward.append((count - 1, 0))
        backward = [(target, source) for source, target in forward]
        low = lax.ppermute(
            lax.slice_in_dim(block, block.shape[dim] - width, None, axis=dim), axis, forward
        )
        high = lax.ppermute(lax.slice_in_dim(block, 0, width, axis=dim), axis, backward)
        block = jnp.concatenate([low, block, high], axis=dim)
    return block


def silu_slope(values):
    sigmoid_part = jax.nn.sigmoid(values)
    return sigmoid_part * (1.0 + values * (1.0 - sigmoid_part))


def radial(source, target, factor, filters):
    square = jnp.zeros((source.shape[1], target.shape[1]), jnp.float32)
    for component in range(3):
        offset = source[component][:, None] - target[component][None, :]
        square = square + offset * offset
    distance = jnp.sqrt(square + 0.01)
    envelope = jnp.where(distance < CUTOFF, 0.5 * (jnp.cos(jnp.pi * distance / CUTOFF) + 1.0), 0.0)
    centers = jnp.arange(filters).astype(jnp.float32) * SPACING
    shifted = (distance[None] - centers[:, None, None]) / SPREAD
    return (jnp.exp(-shifted * shifted) * (envelope * factor)[None]).astype(jnp.bfloat16)


def body(
    atom_feat,
    atom_pos,
    atom_counts,
    atom_nbrs,
    probe_pos,
    probe_target,
    tile_blocks,
    atom_filter,
    probe_filter,
    mix_weight,
    readout,
):
    highest = lax.Precision.HIGHEST
    blocks_dev, channels, atom_width = atom_feat.shape
    tiles_dev, reads_tile = tile_blocks.shape
    probe_count = probe_pos.shape[2]
    filters = atom_filter.shape[1] // channels
    nbr_count = atom_nbrs.shape[1]
    tile_peers = lax.axis_size("tile")
    space_count = lax.axis_size("space")
    space_here = lax.axis_index("space")
    atom_mask = (jnp.arange(atom_width)[None, :] < atom_counts[:, None]).astype(jnp.float32)
    masked_feat = (atom_feat.astype(jnp.float32) * atom_mask[:, None, :]).astype(jnp.bfloat16)
    packed_rows = jnp.concatenate([masked_feat, atom_pos], axis=1)
    around_rows = with_halo(packed_rows, (("space", 0),), blocks_dev)
    side_index = (atom_nbrs // (tile_peers * blocks_dev) - space_here + 1) % space_count
    source_rows = side_index * blocks_dev + atom_nbrs % blocks_dev
    neighbour_rows = jnp.take(around_rows, source_rows.reshape(-1), axis=0).reshape(
        blocks_dev, nbr_count, channels + 3, atom_width
    )
    atom_scale = (nbr_count * atom_width) ** (-0.5)

    def atom_block(inputs):
        picked_rows, own_pos, own_feat, own_mask = inputs
        source_feat = picked_rows[:, :channels]
        source_where = picked_rows[:, channels:].astype(jnp.float32)
        target_where = own_pos.astype(jnp.float32)
        kernel_rows = jax.vmap(lambda source: radial(source, target_where, atom_scale, filters))(
            source_where
        )
        atom_sums = jnp.einsum(
            "kcj,krji->rci", source_feat, kernel_rows, preferred_element_type=jnp.float32
        )
        atom_sums = atom_sums.astype(jnp.bfloat16).reshape(filters * channels, atom_width)
        message = jnp.dot(atom_filter, atom_sums, preferred_element_type=jnp.float32)
        updated = (
            (own_feat.astype(jnp.float32) + jax.nn.silu(message)) * own_mask[None, :]
        ).astype(jnp.bfloat16)
        return (updated, atom_sums, message)

    updated, atom_sums, message = lax.map(
        atom_block, (neighbour_rows, atom_pos, atom_feat, atom_mask)
    )
    stored_rows = jnp.concatenate([updated, atom_pos], axis=1)
    flat_owner = (tile_blocks // blocks_dev % tile_peers).reshape(-1)
    flat_spot = (tile_blocks % blocks_dev).reshape(-1)
    request_cap = max(2, 2 * reads_tile * tiles_dev // tile_peers)
    matches = (flat_owner[:, None, None] == jnp.arange(tile_peers)[None, :, None]) & (
        flat_spot[:, None, None] == jnp.arange(blocks_dev)[None, None, :]
    )
    needed_rows = jnp.any(matches, axis=0).astype(jnp.int32)
    rank_rows = jnp.cumsum(needed_rows, axis=1) - needed_rows
    chosen_rows = (needed_rows[:, None, :] == 1) & (
        rank_rows[:, None, :] == jnp.arange(request_cap)[None, :, None]
    )
    request_ids = jnp.sum(
        chosen_rows.astype(jnp.int32) * jnp.arange(blocks_dev)[None, None, :], axis=2
    )
    asked_ids = lax.all_to_all(request_ids, "tile", split_axis=0, concat_axis=0, tiled=True)
    sent_rows = jnp.take(stored_rows, asked_ids, axis=0)
    replies, asked_ids = (
        lax.all_to_all(sent_rows, "tile", split_axis=0, concat_axis=0, tiled=True),
        asked_ids,
    )
    slot_index = flat_owner * request_cap + rank_rows[flat_owner, flat_spot]
    slot_total = tile_peers * request_cap
    fetched = jnp.take(replies.reshape(slot_total, channels + 3, atom_width), slot_index, axis=0)
    fetched = fetched.reshape(tiles_dev, reads_tile, channels + 3, atom_width)
    probe_scale = (reads_tile * atom_width) ** (-0.5)

    def probe_tile(tile_index):
        tile_fetch = fetched[tile_index]
        probe_where = probe_pos[tile_index]
        source_where = tile_fetch[:, channels:].astype(jnp.float32)
        kernels = jax.vmap(lambda source: radial(source, probe_where, probe_scale, filters))(
            source_where
        )
        summed = jnp.einsum(
            "kca,krap->rcp", tile_fetch[:, :channels], kernels, preferred_element_type=jnp.float32
        )
        summed = summed.astype(jnp.bfloat16).reshape(filters * channels, probe_count)
        hidden = jnp.dot(probe_filter, summed, preferred_element_type=jnp.float32)
        squashed = jax.nn.silu(hidden).astype(jnp.bfloat16)
        mixed_rows = jnp.dot(mix_weight, squashed, preferred_element_type=jnp.float32)
        outer_act = jax.nn.silu(mixed_rows)
        density = jnp.dot(readout, outer_act, precision=highest)
        misfit = (density - probe_target[tile_index]) / probe_count
        grad_readout = jnp.dot(outer_act, misfit, precision=highest)
        grad_mixed = (readout[:, None] * misfit[None, :] * silu_slope(mixed_rows)).astype(
            jnp.bfloat16
        )
        grad_mix = jnp.dot(grad_mixed, squashed.T, preferred_element_type=jnp.float32)
        grad_squashed = jnp.dot(mix_weight.T, grad_mixed, preferred_element_type=jnp.float32)
        grad_hidden = (grad_squashed * silu_slope(hidden)).astype(jnp.bfloat16)
        grad_probe = jnp.dot(grad_hidden, summed.T, preferred_element_type=jnp.float32)
        grad_summed = jnp.dot(probe_filter.T, grad_hidden, preferred_element_type=jnp.float32)
        grad_summed = grad_summed.astype(jnp.bfloat16).reshape(filters, channels, probe_count)
        grad_blocks = jnp.einsum(
            "rcp,krap->kca", grad_summed, kernels, preferred_element_type=jnp.float32
        )
        return (density, grad_probe, grad_mix, grad_readout, grad_blocks)

    density, grad_probe, grad_mix, grad_readout, grad_blocks = lax.map(
        probe_tile, jnp.arange(tiles_dev)
    )
    grad_flat = grad_blocks.reshape(tiles_dev * reads_tile, channels, atom_width)
    pick_rows = (slot_index[None, :] == jnp.arange(slot_total)[:, None]).astype(jnp.float32)
    slot_grad = jnp.einsum("gs,sca->gca", pick_rows, grad_flat, precision=highest).astype(
        jnp.bfloat16
    )
    returned = lax.all_to_all(
        slot_grad.reshape(tile_peers, request_cap, channels, atom_width),
        "tile",
        split_axis=0,
        concat_axis=0,
        tiled=True,
    )
    owner_pick = (asked_ids[:, :, None] == jnp.arange(blocks_dev)[None, None, :]).astype(
        jnp.float32
    )
    block_grad = jnp.einsum(
        "tkb,tkca->bca", owner_pick, returned.astype(jnp.float32), precision=highest
    )
    grad_message = (block_grad * atom_mask[:, None, :] * silu_slope(message)).astype(jnp.bfloat16)
    grad_atom = jnp.einsum(
        "bca,bda->cd", grad_message, atom_sums, preferred_element_type=jnp.float32
    )
    totals = lax.psum(
        (
            grad_atom,
            jnp.sum(grad_probe, axis=0),
            jnp.sum(grad_mix, axis=0),
            jnp.sum(grad_readout, axis=0),
        ),
        ("space", "tile"),
    )
    return (density, totals[0], totals[1], totals[2], totals[3])


def solution(mesh):
    return jax.shard_map(
        body,
        mesh=mesh,
        in_specs=(
            P(("space", "tile"), None, None),
            P(("space", "tile"), None, None),
            P(("space", "tile")),
            P(("space", "tile"), None),
            P(("space", "tile"), None, None),
            P(("space", "tile"), None),
            P(("space", "tile"), None),
            P(),
            P(),
            P(),
            P(),
        ),
        out_specs=(P(("space", "tile"), None), P(), P(), P(), P()),
        check_vma=False,
    )
```

profile of v0, /device:TPU:0, one launch (start us, length us, event | category | flops | bytes accessed | tf_op | source)
XLA Modules:
  0.0 433.7 jit_solution(2652389257295615800)
XLA Ops:
  14.0 5.8 %all-to-all-start = ((s32[8,1,4]{2,1,0:T(1,128)}), s32[8,1,4]{2,1,0:T(1,128)S(1)}, u32[]{:S(2)}, u32[]{:S(2)}) async-start(s32[8,1,4]{2,1,0:T(1,128)} %copy.115), calls=%async_computation | async-start | bytes 8192 | tf_op jit(solution)/shard_map/all_to_all | solution.py:111
  20.2 6.0 %all-to-all-done = s32[8,1,4]{2,1,0:T(1,128)S(1)} async-done(((s32[8,1,4]{2,1,0:T(1,128)}), s32[8,1,4]{2,1,0:T(1,128)S(1)}, u32[]{:S(2)}, u32[]{:S(2)}) %all-to-all-start) | async-done | bytes 160 | tf_op jit(solution)/shard_map/all_to_all | solution.py:111
  31.6 114.4 %while.36 = (s32[]{:T(128)}, bf16[16,128,128]{2,1,0:T(8,128)(2,1)S(1)}, bf16[16,1024,128]{2,1,0:T(8,128)(2,1)}, f32[16,128,128]{2,0,1:T(8,128)}, bf16[16,128,128...) while((s32[]{:T(128)}, ...), condition=%wide.region_4.5_spmd, body=%wide.region_3.4_spmd.sunk | while | flops 172165008 | bytes 3516337 | solution.py:93
  35.8 2.9 dynamic_update_slice.71
  43.0 2.9 dynamic_update_slice.71
  50.1 2.9 dynamic_update_slice.71
  57.3 2.9 dynamic_update_slice.71
  64.4 2.9 dynamic_update_slice.71
  71.6 2.9 dynamic_update_slice.71
  78.8 2.9 dynamic_update_slice.71
  85.9 2.9 dynamic_update_slice.71
  149.0 5.3 %all-to-all-start.1 = ((bf16[8,4,131,128]{3,1,2,0:T(4,128)(2,1)}), bf16[8,4,131,128]{3,1,2,0:T(4,128)(2,1)S(1)}, u32[]{:S(2)}, u32[]{:S(2)}) async-start(bf16[8,4,131,128]{3,1,2,0:T(4,128)(2,1)} %copy.129), calls=%async_computation.1 | async-start | bytes 2146304 | tf_op jit(solution)/shard_map/all_to_all | solution.py:114
  155.8 24.4 %all-to-all-done.1 = bf16[8,4,131,128]{3,1,2,0:T(4,128)(2,1)S(1)} async-done(((bf16[8,4,131,128]{3,1,2,0:T(4,128)(2,1)}), bf16[8,4,131,128]{3,1,2,0:T(4,128)(2,1)S(1)}, u32[]{:S(2)}, u32[]{:S(2)}) %all-to-all-start.1) | async-done | bytes 1073184 | tf_op jit(solution)/shard_map/all_to_all | solution.py:114
  182.0 70.0 %while.37 = (s32[]{:T(128)}, f32[2,512]{1,0:T(2,128)S(1)}, f32[2,128,1024]{2,1,0:T(8,128)}, f32[2,128,128]{2,1,0:T(8,128)}, f32[2,128]{1,0:T(2,128)}, /*index=5*...) while((s32[]{:T(128)}, f32[2,512]{1,0:T(2,128)S(1)}, ...), condition=%wide.region_6.7_spmd, body=%wide.region_5.6_spmd.sunk | while | flops 2663714816 | bytes 38164880 | solution.py:155
  185.8 8.5 %add_sqrt_fusion.5 = (f32[8,128,512]{2,1,0:T(8,128)S(1)}, f32[8,128,512]{2,1,0:T(8,128)S(1)}) fusion(f32[512]{0:T(512)S(1)} %bitcast.288, f32[8,128]{1,0:T(8,128)S(1)} %bitcast.284, f32[512]{0:T(512)S(1)} %bitcast.287, f32[8,128]{1,0:T(8,128)S(1)} %bitcast.285, f32[512]{0:T(512)S(1)} %bitcast.286, f32[8,128]{1,0:T(8,128)S(1)} %bitcast.283), kind=kLoop, calls=%fused_computation.47.clone.2 | loop fusion | flops 7864320 | bytes 4212736 | tf_op jit(solution)/shard_map/while/body/eval_jaxpr/vmap()/sqrt | solution.py:35
  194.3 5.1 %bitcast_convert_fusion.2 = bf16[8,512,128]{1,2,0:T(8,128)(2,1)S(1)} fusion(f32[8,128,512]{2,1,0:T(8,128)S(1)} %get-tuple-element.580, f32[8]{0:T(128)S(1)} %convert_multiply_fusion.5, f32[8,128,512]{2,1,0:T(8,128)S(1)} %get-tuple-element.581, bf16[8,131,128]{2,1,0:T(8,128)(2,1)S(1)} %dynamic-slice_bitcast_fusion.5), kind=kOutput, calls=%fused_computation.45.clone.1 | convolution fusion | flops 1099431936 | bytes 5505536 | tf_op jit(solution)/shard_map/while/body/eval_jaxpr/kca,krap->rcp/dot_general | solution.py:130
  210.0 7.0 %fusion.163 = f32[2,8,128,128]{2,3,1,0:T(8,128)} fusion(f32[2,8,128,128]{2,3,1,0:T(8,128)} %get-tuple-element.638, s32[]{:T(128)S(6)} %copy.188, bf16[8,128,512,1]{2,1,0,3:T(8,128)(2,1)} %bitcast.273, f32[8,128,512]{2,1,0:T(8,128)} %copy-done, f32[8]{0:T(128)} %copy-done.31, f32[8,128,512]{2,1,0:T(8,128)S(1)} %get-tuple-element.581), kind=kOutput, calls=%fused_computation.51.clone.1 | convolution fusion | flops 1098907648 | bytes 5767684 | tf_op jit(solution)/shard_map/while/body/eval_jaxpr/rcp,krap->kca/dot_general | solution.py:150
  220.6 8.5 %add_sqrt_fusion.5 = (f32[8,128,512]{2,1,0:T(8,128)S(1)}, f32[8,128,512]{2,1,0:T(8,128)S(1)}) fusion(f32[512]{0:T(512)S(1)} %bitcast.288, f32[8,128]{1,0:T(8,128)S(1)} %bitcast.284, f32[512]{0:T(512)S(1)} %bitcast.287, f32[8,128]{1,0:T(8,128)S(1)} %bitcast.285, f32[512]{0:T(512)S(1)} %bitcast.286, f32[8,128]{1,0:T(8,128)S(1)} %bitcast.283), kind=kLoop, calls=%fused_computation.47.clone.2 | loop fusion | flops 7864320 | bytes 4212736 | tf_op jit(solution)/shard_map/while/body/eval_jaxpr/vmap()/sqrt | solution.py:35
  229.1 5.1 %bitcast_convert_fusion.2 = bf16[8,512,128]{1,2,0:T(8,128)(2,1)S(1)} fusion(f32[8,128,512]{2,1,0:T(8,128)S(1)} %get-tuple-element.580, f32[8]{0:T(128)S(1)} %convert_multiply_fusion.5, f32[8,128,512]{2,1,0:T(8,128)S(1)} %get-tuple-element.581, bf16[8,131,128]{2,1,0:T(8,128)(2,1)S(1)} %dynamic-slice_bitcast_fusion.5), kind=kOutput, calls=%fused_computation.45.clone.1 | convolution fusion | flops 1099431936 | bytes 5505536 | tf_op jit(solution)/shard_map/while/body/eval_jaxpr/kca,krap->rcp/dot_general | solution.py:130
  244.8 7.0 %fusion.163 = f32[2,8,128,128]{2,3,1,0:T(8,128)} fusion(f32[2,8,128,128]{2,3,1,0:T(8,128)} %get-tuple-element.638, s32[]{:T(128)S(6)} %copy.188, bf16[8,128,512,1]{2,1,0,3:T(8,128)(2,1)} %bitcast.273, f32[8,128,512]{2,1,0:T(8,128)} %copy-done, f32[8]{0:T(128)} %copy-done.31, f32[8,128,512]{2,1,0:T(8,128)S(1)} %get-tuple-element.581), kind=kOutput, calls=%fused_computation.51.clone.1 | convolution fusion | flops 1098907648 | bytes 5767684 | tf_op jit(solution)/shard_map/while/body/eval_jaxpr/rcp,krap->kca/dot_general | solution.py:150
  256.4 3.7 all-to-all-start.2
  261.8 24.1 %all-to-all-done.2 = bf16[8,4,128,128]{3,1,2,0:T(4,128)(2,1)S(1)} async-done(((bf16[8,4,128,128]{3,1,2,0:T(4,128)(2,1)}), bf16[8,4,128,128]{3,1,2,0:T(4,128)(2,1)S(1)}, u32[]{:S(2)}, u32[]{:S(2)}) %all-to-all-start.2) | async-done | bytes 1048608 | tf_op jit(solution)/shard_map/all_to_all | solution.py:163
  290.4 38.8 %psum.31 = f32[128]{0:T(128)} all-reduce(f32[128]{0:T(128)S(1)} %reduce_sum.39), channel_id=1, replica_groups=mesh['space'=4,'tile'=8] {'space','tile'}, use_global_device_ids=true, to_apply=%region_13.14 | all-reduce | flops 128 | bytes 1024 | tf_op jit(solution)/shard_map/psum | solution.py:180
  329.2 93.2 %all-reduce.3.cloned.1.call-done = (f32[128,1024]{1,0:T(8,128)}, f32[128,1024]{1,0:T(8,128)}, f32[128,128]{1,0:T(8,128)}) async-done(((f32[128,1024]{1,0:T(8,128)}, f32[128,1024]{1,0:T(8,128)}, f32[128,128]{1,0:T(8,128)}), (f32[128,1024]{1,0:T(8,128)}, f32[128,1024]{1,0:T(8,128)}, f32[128,128]{1,0:T(8,128)})) %all-reduce.3.cloned.1.call-update) | async-done | bytes 1114128 | tf_op jit(solution)/shard_map/psum | solution.py:180
  (488 shorter events, 147.0 us)
Async XLA Ops:
  7.2 12.7 %copy-start.10 = (bf16[16,3,128]{2,0,1:T(8,128)(2,1)S(1)}, bf16[16,3,128]{2,0,1:T(8,128)(2,1)}, u32[]{:S(2)}) copy-start(bf16[16,3,128]{2,0,1:T(8,128)(2,1)} %param.16) | copy-start | bytes 36868
  7.2 12.7 %copy-start.17 = (s32[16,4]{0,1:T(4,128)S(1)}, s32[16,4]{0,1:T(4,128)}, u32[]{:S(2)}) copy-start(s32[16,4]{0,1:T(4,128)} %param.18) | copy-start | bytes 772
  10.1 16.5 %collective-permute-start.1 = (bf16[16,131,128]{2,0,1:T(8,128)(2,1)S(1)}, bf16[16,131,128]{2,0,1:T(8,128)(2,1)S(1)}, u32[]{:S(2)}, u32[]{:S(2)}) collective-permute-start(bf16[16,131,128]{2,0,1:T(8,128)(2,1)S(1)} %pad_maximum_fusion.2), channel_id=1, source_target_pairs={{8,0},{16,8},{24,16},{0,24},{9,1},{17,9},{25,17},{1,25},{10,2},{18... | collective-permute-start | bytes 1609736 | tf_op jit(solution)/shard_map/ppermute | solution.py:20
  12.5 14.1 %collective-permute-start = (bf16[16,131,128]{2,0,1:T(8,128)(2,1)S(1)}, bf16[16,131,128]{2,0,1:T(8,128)(2,1)S(1)}, u32[]{:S(2)}, u32[]{:S(2)}) collective-permute-start(bf16[16,131,128]{2,0,1:T(8,128)(2,1)S(1)} %pad_maximum_fusion.2), channel_id=1, source_target_pairs={{0,8},{8,16},{16,24},{24,0},{1,9},{9,17},{17,25},{25,1},{2,10},{10... | collective-permute-start | bytes 1609736 | tf_op jit(solution)/shard_map/ppermute | solution.py:17
  14.0 12.3 %all-to-all-start = ((s32[8,1,4]{2,1,0:T(1,128)}), s32[8,1,4]{2,1,0:T(1,128)S(1)}, u32[]{:S(2)}, u32[]{:S(2)}) async-start(s32[8,1,4]{2,1,0:T(1,128)} %copy.115), calls=%async_computation | async-start | bytes 8192 | tf_op jit(solution)/shard_map/all_to_all | solution.py:111
  149.0 31.2 %all-to-all-start.1 = ((bf16[8,4,131,128]{3,1,2,0:T(4,128)(2,1)}), bf16[8,4,131,128]{3,1,2,0:T(4,128)(2,1)S(1)}, u32[]{:S(2)}, u32[]{:S(2)}) async-start(bf16[8,4,131,128]{3,1,2,0:T(4,128)(2,1)} %copy.129), calls=%async_computation.1 | async-start | bytes 2146304 | tf_op jit(solution)/shard_map/all_to_all | solution.py:114
  155.8 26.2 %copy-start.1 = (bf16[128,1024]{1,0:T(8,128)(2,1)S(1)}, bf16[128,1024]{1,0:T(8,128)(2,1)}, u32[]{:S(2)}) copy-start(bf16[128,1024]{1,0:T(8,128)(2,1)} %param.23) | copy-start | bytes 786436
  155.8 26.2 %copy-start.11 = (f32[2,3,512]{2,0,1:T(2,128)S(1)}, f32[2,3,512]{2,0,1:T(2,128)}, u32[]{:S(2)}) copy-start(f32[2,3,512]{2,0,1:T(2,128)} %param.19) | copy-start | bytes 36868
  155.8 26.2 %copy-start.15 = (f32[128]{0:T(128)S(1)}, f32[128]{0:T(128)}, u32[]{:S(2)}) copy-start(f32[128]{0:T(128)} %param.25) | copy-start | bytes 1540
  155.8 26.2 %copy-start.24 = (bf16[128,128]{1,0:T(8,128)(2,1)S(1)}, bf16[128,128]{1,0:T(8,128)(2,1)}, u32[]{:S(2)}) copy-start(bf16[128,128]{1,0:T(8,128)(2,1)} %param.24) | copy-start | bytes 98308
  182.2 12.1 %copy-start.29 = (s32[2]{0:T(128)}, s32[2]{0:T(128)S(1)}, u32[]{:S(2)}) copy-start(s32[2]{0:T(128)S(1)} %get-tuple-element.657) | copy-start | bytes 28 | tf_op jit(solution)/shard_map/while
  210.0 7.0 %copy-start.16 = (f32[128]{0:T(128)S(1)}, f32[128]{0:T(128)}, u32[]{:S(2)}) copy-start(f32[128]{0:T(128)} %get-tuple-element.715) | copy-start | bytes 1540 | tf_op jit(solution)/shard_map/while
  210.0 7.0 %copy-start.25 = (bf16[128,128]{1,0:T(8,128)(2,1)S(1)}, bf16[128,128]{1,0:T(8,128)(2,1)}, u32[]{:S(2)}) copy-start(bf16[128,128]{1,0:T(8,128)(2,1)} %get-tuple-element.735) | copy-start | bytes 98308 | tf_op jit(solution)/shard_map/while
  210.0 7.0 %copy-start.27 = (f32[2,512]{1,0:T(2,128)S(1)}, f32[2,512]{1,0:T(2,128)}, u32[]{:S(2)}) copy-start(f32[2,512]{1,0:T(2,128)} %copy-done.26) | copy-start | bytes 12292 | tf_op jit(solution)/shard_map/while
  210.0 7.0 %copy-start.30 = (s32[2]{0:T(128)S(1)}, s32[2]{0:T(128)}, u32[]{:S(2)}) copy-start(s32[2]{0:T(128)} %copy-done.29) | copy-start | bytes 28 | tf_op jit(solution)/shard_map/while
  217.0 12.1 %copy-start.29 = (s32[2]{0:T(128)}, s32[2]{0:T(128)S(1)}, u32[]{:S(2)}) copy-start(s32[2]{0:T(128)S(1)} %get-tuple-element.657) | copy-start | bytes 28 | tf_op jit(solution)/shard_map/while
  244.8 7.0 %copy-start.16 = (f32[128]{0:T(128)S(1)}, f32[128]{0:T(128)}, u32[]{:S(2)}) copy-start(f32[128]{0:T(128)} %get-tuple-element.715) | copy-start | bytes 1540 | tf_op jit(solution)/shard_map/while
  244.8 7.0 %copy-start.25 = (bf16[128,128]{1,0:T(8,128)(2,1)S(1)}, bf16[128,128]{1,0:T(8,128)(2,1)}, u32[]{:S(2)}) copy-start(bf16[128,128]{1,0:T(8,128)(2,1)} %get-tuple-element.735) | copy-start | bytes 98308 | tf_op jit(solution)/shard_map/while
  244.8 7.0 %copy-start.27 = (f32[2,512]{1,0:T(2,128)S(1)}, f32[2,512]{1,0:T(2,128)}, u32[]{:S(2)}) copy-start(f32[2,512]{1,0:T(2,128)} %copy-done.26) | copy-start | bytes 12292 | tf_op jit(solution)/shard_map/while
  244.8 7.0 %copy-start.30 = (s32[2]{0:T(128)S(1)}, s32[2]{0:T(128)}, u32[]{:S(2)}) copy-start(s32[2]{0:T(128)} %copy-done.29) | copy-start | bytes 28 | tf_op jit(solution)/shard_map/while
  256.4 29.5 %copy-start.14 = (f32[16,128]{1,0:T(8,128)S(1)}, f32[16,128]{1,0:T(8,128)}, u32[]{:S(2)}) copy-start(f32[16,128]{1,0:T(8,128)} %copy-done.13) | copy-start | bytes 24580
  256.4 29.5 %copy-start.23 = (f32[16,128,128]{2,0,1:T(8,128)S(1)}, f32[16,128,128]{2,0,1:T(8,128)}, u32[]{:S(2)}) copy-start(f32[16,128,128]{2,0,1:T(8,128)} %get-tuple-element.288) | copy-start | bytes 3145732
  256.4 29.5 %all-to-all-start.2 = ((bf16[8,4,128,128]{3,1,2,0:T(4,128)(2,1)}), bf16[8,4,128,128]{3,1,2,0:T(4,128)(2,1)S(1)}, u32[]{:S(2)}, u32[]{:S(2)}) async-start(bf16[8,4,128,128]{3,1,2,0:T(4,128)(2,1)} %copy.133), calls=%async_computation.2 | async-start | bytes 2097152 | tf_op jit(solution)/shard_map/all_to_all | solution.py:163
  260.1 162.3 %all-reduce.3.cloned.1.call-start = ((), (), s32[]{:S(2)}) async-start(), calls=%async_computation.3 | async-start | bytes 2228224 | tf_op jit(solution)/shard_map/psum | solution.py:180
  (28 other events, 75.4 us)
Sparse Core Ops, SparseCore 0:
  290.5 131.8 all-reduce.2
where the time goes:
time: 436 us; the launch traced here: 434 us
  waiting for transfers between devices  148 us (34%)
  local copies, waits for them, and re-layouts  105 us (24%)
  matrix products  55.9 us (13%)
  other arithmetic  47.9 us (11%)
  blocking collectives  38.8 us (9%)
  starting transfers between devices  17.4 us (4%)
  between operations  14.4 us (3%)
  loops' own time  6.15 us (1%)
    psum x1, waiting for transfers between devices, body(): lax.psum((grad_atom, jnp.sum(grad_probe, axis=0), jnp.sum(grad_mix, axis=...  93.2 us
    dynamic_update_slice x80, local copies, waits for them, and re-layouts, body(): lax.map(atom_block, (neighbour_rows, atom_pos, atom_feat, atom_mask))  62.2 us
    psum x1, blocking collectives, body(): lax.psum((grad_atom, jnp.sum(grad_probe, axis=0), jnp.sum(grad_mix, axis=...  38.8 us
    sqrt x18, other arithmetic, radial(): distance = jnp.sqrt(square + 0.01)  34.7 us
    all_to_all x1, waiting for transfers between devices, body(): lax.all_to_all(sent_rows, 'tile', split_axis=0, concat_axis=0, tiled=True)  24.4 us
    all_to_all x1, waiting for transfers between devices, body(): lax.all_to_all(slot_grad.reshape(tile_peers, request_cap, channels, atom_...  24.1 us
    dynamic_slice x32, local copies, waits for them, and re-layouts, body(): lax.map(atom_block, (neighbour_rows, atom_pos, atom_feat, atom_mask))  14 us
    dot_general x2, matrix products, probe_tile(): jnp.einsum('rcp,krap->kca', grad_summed, kernels, preferred_element_type=...  14 us
  transfers between devices with their start and end apart: 6, of which 4 were waited for; matrix products, arithmetic and copies ran while one was open for 1% of the time, Pallas kernels for 0%

commit v1 on v0

--- a/solution.py
+++ b/solution.py
@@ -178,13 +178,16 @@
         "bca,bda->cd", grad_message, atom_sums, preferred_element_type=jnp.float32
     )
     totals = lax.psum(
-        (
-            grad_atom,
-            jnp.sum(grad_probe, axis=0),
-            jnp.sum(grad_mix, axis=0),
-            jnp.sum(grad_readout, axis=0),
+        lax.psum(
+            (
+                grad_atom,
+                jnp.sum(grad_probe, axis=0),
+                jnp.sum(grad_mix, axis=0),
+                jnp.sum(grad_readout, axis=0),
+            ),
+            "tile",
         ),
-        ("space", "tile"),
+        "space",
     )
     return (density, totals[0], totals[1], totals[2], totals[3])
 

time: 436 us -> 422 us (0.968)
  blocking collectives: 38.8 us -> 26.1 us
    psum x1, blocking collectives: 38.8 us -> 19.9 us  [body(): lax.psum((grad_atom, jnp.sum(grad_probe, axis=0), jnp.sum(grad_mix, axis=...]
    psum x1, waiting for transfers between devices: 93.2 us -> 79.4 us  [body(): lax.psum((grad_atom, jnp.sum(grad_probe, axis=0), jnp.sum(grad_mix, axis=...]
    psum x0 -> x1, waiting for transfers between devices: none -> 12.9 us  [body(): lax.psum(lax.psum((grad_atom, jnp.sum(grad_probe, axis=0), jnp.sum(grad_m...]
    psum x0 -> x1, blocking collectives: none -> 6.15 us  [body(): lax.psum(lax.psum((grad_atom, jnp.sum(grad_probe, axis=0), jnp.sum(grad_m...]
  transfers between devices with their start and end apart: 6 -> 7, of which waited for: 4 -> 5; matrix products, arithmetic and copies ran while one was open for 1% -> 1% of each run, Pallas kernels for 0% -> 0%
where the time goes in v1:
time: 422 us; the launch traced here: 420 us
  waiting for transfers between devices  147 us (35%)
  local copies, waits for them, and re-layouts  105 us (25%)
  matrix products  55.9 us (13%)
  other arithmetic  47.9 us (11%)
  blocking collectives  26.1 us (6%)
  starting transfers between devices  17.4 us (4%)
  between operations  14.4 us (3%)
  loops' own time  6.16 us (1%)
    psum x1, waiting for transfers between devices, body(): lax.psum((grad_atom, jnp.sum(grad_probe, axis=0), jnp.sum(grad_mix, axis=...  79.4 us
    dynamic_update_slice x80, local copies, waits for them, and re-layouts, body(): lax.map(atom_block, (neighbour_rows, atom_pos, atom_feat, atom_mask))  62.1 us
    sqrt x18, other arithmetic, radial(): distance = jnp.sqrt(square + 0.01)  34.7 us
    all_to_all x1, waiting for transfers between devices, body(): lax.all_to_all(sent_rows, 'tile', split_axis=0, concat_axis=0, tiled=True)  24.4 us
    all_to_all x1, waiting for transfers between devices, body(): lax.all_to_all(slot_grad.reshape(tile_peers, request_cap, channels, atom_...  24.1 us
    psum x1, blocking collectives, body(): lax.psum((grad_atom, jnp.sum(grad_probe, axis=0), jnp.sum(grad_mix, axis=...  19.9 us
    dynamic_slice x32, local copies, waits for them, and re-layouts, body(): lax.map(atom_block, (neighbour_rows, atom_pos, atom_feat, atom_mask))  14 us
    dot_general x2, matrix products, probe_tile(): jnp.einsum('rcp,krap->kca', grad_summed, kernels, preferred_element_type=...  13.9 us
  transfers between devices with their start and end apart: 7, of which 5 were waited for; matrix products, arithmetic and copies ran while one was open for 1% of the time, Pallas kernels for 0%

profile of v1, /device:TPU:0, one launch (start us, length us, event | category | flops | bytes accessed | tf_op | source)
XLA Modules:
  0.0 420.0 jit_solution(3685510557698415716)
XLA Ops:
  14.0 5.8 %all-to-all-start = ((s32[8,1,4]{2,1,0:T(1,128)}), s32[8,1,4]{2,1,0:T(1,128)S(1)}, u32[]{:S(2)}, u32[]{:S(2)}) async-start(s32[8,1,4]{2,1,0:T(1,128)} %copy.115), calls=%async_computation | async-start | bytes 8192 | tf_op jit(solution)/shard_map/all_to_all | solution.py:111
  20.2 6.0 %all-to-all-done = s32[8,1,4]{2,1,0:T(1,128)S(1)} async-done(((s32[8,1,4]{2,1,0:T(1,128)}), s32[8,1,4]{2,1,0:T(1,128)S(1)}, u32[]{:S(2)}, u32[]{:S(2)}) %all-to-all-start) | async-done | bytes 160 | tf_op jit(solution)/shard_map/all_to_all | solution.py:111
  31.6 114.4 %while.36 = (s32[]{:T(128)}, bf16[16,128,128]{2,1,0:T(8,128)(2,1)S(1)}, bf16[16,1024,128]{2,1,0:T(8,128)(2,1)}, f32[16,128,128]{2,0,1:T(8,128)}, bf16[16,128,128...) while((s32[]{:T(128)}, ...), condition=%wide.region_4.5_spmd, body=%wide.region_3.4_spmd.sunk | while | flops 172165008 | bytes 3516337 | solution.py:93
  35.8 2.9 dynamic_update_slice.71
  43.0 2.9 dynamic_update_slice.71
  50.2 2.9 dynamic_update_slice.71
  57.3 2.9 dynamic_update_slice.71
  64.5 2.9 dynamic_update_slice.71
  85.9 2.9 dynamic_update_slice.71
  148.9 5.3 %all-to-all-start.1 = ((bf16[8,4,131,128]{3,1,2,0:T(4,128)(2,1)}), bf16[8,4,131,128]{3,1,2,0:T(4,128)(2,1)S(1)}, u32[]{:S(2)}, u32[]{:S(2)}) async-start(bf16[8,4,131,128]{3,1,2,0:T(4,128)(2,1)} %copy.129), calls=%async_computation.1 | async-start | bytes 2146304 | tf_op jit(solution)/shard_map/all_to_all | solution.py:114
  155.7 24.4 %all-to-all-done.1 = bf16[8,4,131,128]{3,1,2,0:T(4,128)(2,1)S(1)} async-done(((bf16[8,4,131,128]{3,1,2,0:T(4,128)(2,1)}), bf16[8,4,131,128]{3,1,2,0:T(4,128)(2,1)S(1)}, u32[]{:S(2)}, u32[]{:S(2)}) %all-to-all-start.1) | async-done | bytes 1073184 | tf_op jit(solution)/shard_map/all_to_all | solution.py:114
  181.9 70.0 %while.37 = (s32[]{:T(128)}, f32[2,512]{1,0:T(2,128)S(1)}, f32[2,128,1024]{2,1,0:T(8,128)}, f32[2,128,128]{2,1,0:T(8,128)}, f32[2,128]{1,0:T(2,128)}, /*index=5*...) while((s32[]{:T(128)}, f32[2,512]{1,0:T(2,128)S(1)}, ...), condition=%wide.region_6.7_spmd, body=%wide.region_5.6_spmd.sunk | while | flops 2663714816 | bytes 38164880 | solution.py:155
  185.7 8.5 %add_sqrt_fusion.5 = (f32[8,128,512]{2,1,0:T(8,128)S(1)}, f32[8,128,512]{2,1,0:T(8,128)S(1)}) fusion(f32[512]{0:T(512)S(1)} %bitcast.288, f32[8,128]{1,0:T(8,128)S(1)} %bitcast.284, f32[512]{0:T(512)S(1)} %bitcast.287, f32[8,128]{1,0:T(8,128)S(1)} %bitcast.285, f32[512]{0:T(512)S(1)} %bitcast.286, f32[8,128]{1,0:T(8,128)S(1)} %bitcast.283), kind=kLoop, calls=%fused_computation.47.clone.2 | loop fusion | flops 7864320 | bytes 4212736 | tf_op jit(solution)/shard_map/while/body/eval_jaxpr/vmap()/sqrt | solution.py:35
  194.2 5.1 %bitcast_convert_fusion.2 = bf16[8,512,128]{1,2,0:T(8,128)(2,1)S(1)} fusion(f32[8,128,512]{2,1,0:T(8,128)S(1)} %get-tuple-element.583, f32[8]{0:T(128)S(1)} %convert_multiply_fusion.5, f32[8,128,512]{2,1,0:T(8,128)S(1)} %get-tuple-element.584, bf16[8,131,128]{2,1,0:T(8,128)(2,1)S(1)} %dynamic-slice_bitcast_fusion.5), kind=kOutput, calls=%fused_computation.45.clone.1 | convolution fusion | flops 1099431936 | bytes 5505536 | tf_op jit(solution)/shard_map/while/body/eval_jaxpr/kca,krap->rcp/dot_general | solution.py:130
  209.9 7.0 %fusion.163 = f32[2,8,128,128]{2,3,1,0:T(8,128)} fusion(f32[2,8,128,128]{2,3,1,0:T(8,128)} %get-tuple-element.641, s32[]{:T(128)S(6)} %copy.188, bf16[8,128,512,1]{2,1,0,3:T(8,128)(2,1)} %bitcast.273, f32[8,128,512]{2,1,0:T(8,128)} %copy-done, f32[8]{0:T(128)} %copy-done.31, f32[8,128,512]{2,1,0:T(8,128)S(1)} %get-tuple-element.584), kind=kOutput, calls=%fused_computation.51.clone.1 | convolution fusion | flops 1098907648 | bytes 5767684 | tf_op jit(solution)/shard_map/while/body/eval_jaxpr/rcp,krap->kca/dot_general | solution.py:150
  220.5 8.5 %add_sqrt_fusion.5 = (f32[8,128,512]{2,1,0:T(8,128)S(1)}, f32[8,128,512]{2,1,0:T(8,128)S(1)}) fusion(f32[512]{0:T(512)S(1)} %bitcast.288, f32[8,128]{1,0:T(8,128)S(1)} %bitcast.284, f32[512]{0:T(512)S(1)} %bitcast.287, f32[8,128]{1,0:T(8,128)S(1)} %bitcast.285, f32[512]{0:T(512)S(1)} %bitcast.286, f32[8,128]{1,0:T(8,128)S(1)} %bitcast.283), kind=kLoop, calls=%fused_computation.47.clone.2 | loop fusion | flops 7864320 | bytes 4212736 | tf_op jit(solution)/shard_map/while/body/eval_jaxpr/vmap()/sqrt | solution.py:35
  229.0 5.1 %bitcast_convert_fusion.2 = bf16[8,512,128]{1,2,0:T(8,128)(2,1)S(1)} fusion(f32[8,128,512]{2,1,0:T(8,128)S(1)} %get-tuple-element.583, f32[8]{0:T(128)S(1)} %convert_multiply_fusion.5, f32[8,128,512]{2,1,0:T(8,128)S(1)} %get-tuple-element.584, bf16[8,131,128]{2,1,0:T(8,128)(2,1)S(1)} %dynamic-slice_bitcast_fusion.5), kind=kOutput, calls=%fused_computation.45.clone.1 | convolution fusion | flops 1099431936 | bytes 5505536 | tf_op jit(solution)/shard_map/while/body/eval_jaxpr/kca,krap->rcp/dot_general | solution.py:130
  244.7 7.0 %fusion.163 = f32[2,8,128,128]{2,3,1,0:T(8,128)} fusion(f32[2,8,128,128]{2,3,1,0:T(8,128)} %get-tuple-element.641, s32[]{:T(128)S(6)} %copy.188, bf16[8,128,512,1]{2,1,0,3:T(8,128)(2,1)} %bitcast.273, f32[8,128,512]{2,1,0:T(8,128)} %copy-done, f32[8]{0:T(128)} %copy-done.31, f32[8,128,512]{2,1,0:T(8,128)S(1)} %get-tuple-element.584), kind=kOutput, calls=%fused_computation.51.clone.1 | convolution fusion | flops 1098907648 | bytes 5767684 | tf_op jit(solution)/shard_map/while/body/eval_jaxpr/rcp,krap->kca/dot_general | solution.py:150
  256.3 3.7 all-to-all-start.2
  261.7 24.1 %all-to-all-done.2 = bf16[8,4,128,128]{3,1,2,0:T(4,128)(2,1)S(1)} async-done(((bf16[8,4,128,128]{3,1,2,0:T(4,128)(2,1)}), bf16[8,4,128,128]{3,1,2,0:T(4,128)(2,1)S(1)}, u32[]{:S(2)}, u32[]{:S(2)}) %all-to-all-start.2) | async-done | bytes 1048608 | tf_op jit(solution)/shard_map/all_to_all | solution.py:163
  290.3 79.4 %all-reduce.5.cloned.1.call-done = (f32[128,1024]{1,0:T(8,128)}, f32[128,1024]{1,0:T(8,128)}, f32[128,128]{1,0:T(8,128)}) async-done(((f32[128,1024]{1,0:T(8,128)}, f32[128,1024]{1,0:T(8,128)}, f32[128,128]{1,0:T(8,128)}), (f32[128,1024]{1,0:T(8,128)}, f32[128,1024]{1,0:T(8,128)}, f32[128,128]{1,0:T(8,128)})) %all-reduce.5.cloned.1.call-update) | async-done | bytes 1114128 | tf_op jit(solution)/shard_map/psum | solution.py:181
  369.7 19.9 %psum.62 = f32[128]{0:T(128)S(1)} all-reduce(f32[128]{0:T(128)S(1)} %reduce_sum.39), channel_id=1, replica_groups=mesh['space'=4,'tile'=8] {'tile'}, use_global_device_ids=true, to_apply=%region_16.17 | all-reduce | flops 128 | bytes 1024 | tf_op jit(solution)/shard_map/psum | solution.py:181
  389.7 6.2 %psum.63 = f32[128]{0:T(128)} all-reduce(f32[128]{0:T(128)S(1)} %psum.62), channel_id=1, replica_groups=mesh['space'=4,'tile'=8] {'space'}, use_global_device_ids=true, to_apply=%region_17.18 | all-reduce | flops 128 | bytes 1024 | tf_op jit(solution)/shard_map/psum | solution.py:180
  395.8 12.9 %all-reduce.7.cloned.1.call-done = (f32[128,1024]{1,0:T(8,128)}, f32[128,1024]{1,0:T(8,128)}, f32[128,128]{1,0:T(8,128)}) async-done(((f32[128,1024]{1,0:T(8,128)}, f32[128,1024]{1,0:T(8,128)}, f32[128,128]{1,0:T(8,128)}), (f32[128,1024]{1,0:T(8,128)}, f32[128,1024]{1,0:T(8,128)}, f32[128,128]{1,0:T(8,128)})) %all-reduce.7.cloned.1.call-update) | async-done | bytes 1114128 | tf_op jit(solution)/shard_map/psum | solution.py:180
  (492 shorter events, 152.8 us)
Async XLA Ops:
  7.2 12.7 %copy-start.10 = (bf16[16,3,128]{2,0,1:T(8,128)(2,1)S(1)}, bf16[16,3,128]{2,0,1:T(8,128)(2,1)}, u32[]{:S(2)}) copy-start(bf16[16,3,128]{2,0,1:T(8,128)(2,1)} %param.16) | copy-start | bytes 36868
  7.2 12.7 %copy-start.17 = (s32[16,4]{0,1:T(4,128)S(1)}, s32[16,4]{0,1:T(4,128)}, u32[]{:S(2)}) copy-start(s32[16,4]{0,1:T(4,128)} %param.18) | copy-start | bytes 772
  10.1 16.5 %collective-permute-start.1 = (bf16[16,131,128]{2,0,1:T(8,128)(2,1)S(1)}, bf16[16,131,128]{2,0,1:T(8,128)(2,1)S(1)}, u32[]{:S(2)}, u32[]{:S(2)}) collective-permute-start(bf16[16,131,128]{2,0,1:T(8,128)(2,1)S(1)} %pad_maximum_fusion.2), channel_id=1, source_target_pairs={{8,0},{16,8},{24,16},{0,24},{9,1},{17,9},{25,17},{1,25},{10,2},{18... | collective-permute-start | bytes 1609736 | tf_op jit(solution)/shard_map/ppermute | solution.py:20
  12.5 14.1 %collective-permute-start = (bf16[16,131,128]{2,0,1:T(8,128)(2,1)S(1)}, bf16[16,131,128]{2,0,1:T(8,128)(2,1)S(1)}, u32[]{:S(2)}, u32[]{:S(2)}) collective-permute-start(bf16[16,131,128]{2,0,1:T(8,128)(2,1)S(1)} %pad_maximum_fusion.2), channel_id=1, source_target_pairs={{0,8},{8,16},{16,24},{24,0},{1,9},{9,17},{17,25},{25,1},{2,10},{10... | collective-permute-start | bytes 1609736 | tf_op jit(solution)/shard_map/ppermute | solution.py:17
  14.0 12.3 %all-to-all-start = ((s32[8,1,4]{2,1,0:T(1,128)}), s32[8,1,4]{2,1,0:T(1,128)S(1)}, u32[]{:S(2)}, u32[]{:S(2)}) async-start(s32[8,1,4]{2,1,0:T(1,128)} %copy.115), calls=%async_computation | async-start | bytes 8192 | tf_op jit(solution)/shard_map/all_to_all | solution.py:111
  148.9 31.2 %all-to-all-start.1 = ((bf16[8,4,131,128]{3,1,2,0:T(4,128)(2,1)}), bf16[8,4,131,128]{3,1,2,0:T(4,128)(2,1)S(1)}, u32[]{:S(2)}, u32[]{:S(2)}) async-start(bf16[8,4,131,128]{3,1,2,0:T(4,128)(2,1)} %copy.129), calls=%async_computation.1 | async-start | bytes 2146304 | tf_op jit(solution)/shard_map/all_to_all | solution.py:114
  155.7 26.2 %copy-start.1 = (bf16[128,1024]{1,0:T(8,128)(2,1)S(1)}, bf16[128,1024]{1,0:T(8,128)(2,1)}, u32[]{:S(2)}) copy-start(bf16[128,1024]{1,0:T(8,128)(2,1)} %param.23) | copy-start | bytes 786436
  155.7 26.2 %copy-start.11 = (f32[2,3,512]{2,0,1:T(2,128)S(1)}, f32[2,3,512]{2,0,1:T(2,128)}, u32[]{:S(2)}) copy-start(f32[2,3,512]{2,0,1:T(2,128)} %param.19) | copy-start | bytes 36868
  155.7 26.2 %copy-start.15 = (f32[128]{0:T(128)S(1)}, f32[128]{0:T(128)}, u32[]{:S(2)}) copy-start(f32[128]{0:T(128)} %param.25) | copy-start | bytes 1540
  155.7 26.2 %copy-start.24 = (bf16[128,128]{1,0:T(8,128)(2,1)S(1)}, bf16[128,128]{1,0:T(8,128)(2,1)}, u32[]{:S(2)}) copy-start(bf16[128,128]{1,0:T(8,128)(2,1)} %param.24) | copy-start | bytes 98308
  182.1 12.1 %copy-start.29 = (s32[2]{0:T(128)}, s32[2]{0:T(128)S(1)}, u32[]{:S(2)}) copy-start(s32[2]{0:T(128)S(1)} %get-tuple-element.660) | copy-start | bytes 28 | tf_op jit(solution)/shard_map/while
  209.9 7.0 %copy-start.27 = (f32[2,512]{1,0:T(2,128)S(1)}, f32[2,512]{1,0:T(2,128)}, u32[]{:S(2)}) copy-start(f32[2,512]{1,0:T(2,128)} %copy-done.26) | copy-start | bytes 12292 | tf_op jit(solution)/shard_map/while
  209.9 7.0 %copy-start.30 = (s32[2]{0:T(128)S(1)}, s32[2]{0:T(128)}, u32[]{:S(2)}) copy-start(s32[2]{0:T(128)} %copy-done.29) | copy-start | bytes 28 | tf_op jit(solution)/shard_map/while
  216.9 12.1 %copy-start.29 = (s32[2]{0:T(128)}, s32[2]{0:T(128)S(1)}, u32[]{:S(2)}) copy-start(s32[2]{0:T(128)S(1)} %get-tuple-element.660) | copy-start | bytes 28 | tf_op jit(solution)/shard_map/while
  244.7 7.0 %copy-start.16 = (f32[128]{0:T(128)S(1)}, f32[128]{0:T(128)}, u32[]{:S(2)}) copy-start(f32[128]{0:T(128)} %get-tuple-element.732) | copy-start | bytes 1540 | tf_op jit(solution)/shard_map/while
  244.7 7.0 %copy-start.25 = (bf16[128,128]{1,0:T(8,128)(2,1)S(1)}, bf16[128,128]{1,0:T(8,128)(2,1)}, u32[]{:S(2)}) copy-start(bf16[128,128]{1,0:T(8,128)(2,1)} %get-tuple-element.752) | copy-start | bytes 98308 | tf_op jit(solution)/shard_map/while
  244.7 7.0 %copy-start.27 = (f32[2,512]{1,0:T(2,128)S(1)}, f32[2,512]{1,0:T(2,128)}, u32[]{:S(2)}) copy-start(f32[2,512]{1,0:T(2,128)} %copy-done.26) | copy-start | bytes 12292 | tf_op jit(solution)/shard_map/while
  244.7 7.0 %copy-start.30 = (s32[2]{0:T(128)S(1)}, s32[2]{0:T(128)}, u32[]{:S(2)}) copy-start(s32[2]{0:T(128)} %copy-done.29) | copy-start | bytes 28 | tf_op jit(solution)/shard_map/while
  256.3 29.5 %copy-start.14 = (f32[16,128]{1,0:T(8,128)S(1)}, f32[16,128]{1,0:T(8,128)}, u32[]{:S(2)}) copy-start(f32[16,128]{1,0:T(8,128)} %copy-done.13) | copy-start | bytes 24580
  256.3 29.5 %copy-start.23 = (f32[16,128,128]{2,0,1:T(8,128)S(1)}, f32[16,128,128]{2,0,1:T(8,128)}, u32[]{:S(2)}) copy-start(f32[16,128,128]{2,0,1:T(8,128)} %get-tuple-element.288) | copy-start | bytes 3145732
  256.3 29.5 %all-to-all-start.2 = ((bf16[8,4,128,128]{3,1,2,0:T(4,128)(2,1)}), bf16[8,4,128,128]{3,1,2,0:T(4,128)(2,1)S(1)}, u32[]{:S(2)}, u32[]{:S(2)}) async-start(bf16[8,4,128,128]{3,1,2,0:T(4,128)(2,1)} %copy.133), calls=%async_computation.2 | async-start | bytes 2097152 | tf_op jit(solution)/shard_map/all_to_all | solution.py:163
  260.0 109.7 %all-reduce.5.cloned.1.call-start = ((), (), s32[]{:S(2)}) async-start(), calls=%async_computation.3 | async-start | bytes 2228224 | tf_op jit(solution)/shard_map/psum | solution.py:181
  290.2 79.5 %copy-start.21 = (f32[2,128]{1,0:T(2,128)S(1)}, f32[2,128]{1,0:T(2,128)}, u32[]{:S(2)}) copy-start(f32[2,128]{1,0:T(2,128)} %get-tuple-element.737) | copy-start | bytes 3076
  290.3 118.4 %all-reduce.7.cloned.1.call-start = ((), (), s32[]{:S(2)}) async-start(), calls=%async_computation.4 | async-start | bytes 2228224 | tf_op jit(solution)/shard_map/psum | solution.py:180
  (29 other events, 87.0 us)
Sparse Core Ops, SparseCore 0:
  290.4 79.2 all-reduce.4
  372.2 36.4 all-reduce.6
